TPU v7x, 256 devices: a whole 4x4x8 slice. The times are simulated.
256 devices in a mesh: pix: 32 (over y, x, core), site: 8 (over z).
Axes of the slice: x: 4, y: 4, z: 8, core: 2. Of those that a mesh axis runs over, the one named last changes fastest.
Arguments:
- margins: int32 [2048, 256, 1024], P('pix', None, 'site'), may hold values from -2047 to 2047
- block_pos: int32 [2048, 8], P('pix', 'site'), may hold values from -1 to 15, as said below
- pattern_ids: int32 [1024], P('site'), may hold values from 0 to 15
- pattern_gain: float32 [16, 256], replicated, may hold values from -4 to 4
- site_price: float32 [1024], P('site'), may hold values from 0.2 to 4
- weights: float32 [131072], P('pix'), may hold values from 0.2 to 2
- site_start: float32 [1024], P('site'), may hold values from 0 to 1
- pixel_start: float32 [131072], P('pix'), may hold values from 0 to 1
- dual_start: float32 [131072], P('pix'), may hold values from 0 to 2
Outputs:
- site_level: float32 [1024], P('site')
- pixel_level: float32 [131072], P('pix')
- duals: float32 [131072], P('pix')
Inputs may be any that keep to these rules, and one draw needn't show every extreme that they name: Row k of block_pos and of margins is held by pixel device k // 64 and belongs to pixel device (k // 2) % 32; its entry for site block b is the position, among that device's 16 pixel blocks, of the pixel block of the tile, or -1 for an empty slot. The lists are filled unevenly. For one pixel device, drawn afresh, every slot that belongs to it is filled in every row group and site block.
All inputs are finite; a program needn't handle non-finite values.
Results may differ from a plain program's by a relative error of at most 0.0003.
Values may be sent and summed in bfloat16 or wider, within the bound.
No kernel may reach another device: no remote copies, remote signals or barrier semaphores. Data moves between devices by JAX's collectives and lax.ppermute only.
A program may use at most 64 MiB of HBM per device.

v0:
```python
import jax
import jax.numpy as jnp
from jax import lax
from jax.sharding import PartitionSpec as P

ITERS = 2
MARGIN_SCALE = 2.0 ** (-9)


def build_tiles(margins, block_pos, pattern_ids, pattern_gain):
    patterns = pattern_gain.shape[0]
    chooser = (pattern_ids[:, None] == jnp.arange(patterns, dtype=jnp.int32)[None, :]).astype(
        jnp.float32
    )
    gain_tile = lax.dot_general(
        pattern_gain, chooser, (((0,), (1,)), ((), ())), precision=lax.Precision.HIGHEST
    )
    filled = block_pos[:, 0] >= 0
    values = jax.nn.sigmoid(margins.astype(jnp.float32) * MARGIN_SCALE + gain_tile[None])
    return jnp.where(filled[:, None, None], values, 0.0).astype(jnp.bfloat16)


def local(
    margins,
    block_pos,
    pattern_ids,
    pattern_gain,
    site_price,
    weights,
    site_start,
    pixel_start,
    dual_start,
):
    slot_count = margins.shape[0]
    block_width = pattern_gain.shape[1]
    blocks = weights.shape[0] // block_width
    coverage = build_tiles(margins, block_pos, pattern_ids, pattern_gain)
    position = block_pos[:, 0]
    tiles_here, arrived = (
        lax.all_to_all(coverage, "pix", split_axis=0, concat_axis=0, tiled=True),
        lax.all_to_all(
            position.astype(jnp.bfloat16), "pix", split_axis=0, concat_axis=0, tiled=True
        ),
    )
    chooser = arrived.astype(jnp.float32)[:, None] == jnp.arange(blocks, dtype=jnp.float32)[None, :]
    chooser_half = chooser.astype(jnp.bfloat16)
    chooser_full = chooser.astype(jnp.float32)

    def spread_rows(products):
        return jnp.einsum("kb,tkr->btr", chooser_full, products, precision=lax.Precision.HIGHEST)

    def column_totals(selected):
        partial_value = jnp.einsum(
            "tkr,krj->tj", selected, tiles_here, preferred_element_type=jnp.float32
        )
        return lax.psum(partial_value, "pix")

    def row_totals(values):
        products = jnp.einsum("krj,tj->tkr", tiles_here, values, preferred_element_type=jnp.float32)
        return lax.psum(spread_rows(products), "site")

    ones_pixels = jnp.ones((1, slot_count, block_width), jnp.bfloat16)
    ones_sites = jnp.ones((1, tiles_here.shape[2]), jnp.bfloat16)
    column_sum = column_totals(ones_pixels)[0]
    row_sum = row_totals(ones_sites)[:, 0, :].reshape(-1)
    site_level, pixel_level, duals = (site_start, pixel_start, dual_start)
    for iteration in range(ITERS):
        dual_half = duals.astype(jnp.bfloat16).reshape(blocks, block_width)
        selected = jnp.dot(chooser_half, dual_half, preferred_element_type=jnp.float32).astype(
            jnp.bfloat16
        )[None]
        pulled = column_totals(selected)[0]
        new_site = jnp.clip(site_level - (site_price - pulled / column_sum), 0.0, 1.0)
        new_pixel = jnp.clip(pixel_level - (duals - weights), 0.0, 1.0)
        extrapolated = (2.0 * new_site - site_level).astype(jnp.bfloat16)[None]
        pushed = row_totals(extrapolated)[:, 0, :].reshape(-1)
        duals = jnp.maximum(duals + (2.0 * new_pixel - pixel_level - pushed) / (row_sum + 1.0), 0.0)
        site_level, pixel_level = (new_site, new_pixel)
    return (site_level, pixel_level, duals)


def solution(mesh):
    placed = (
        P("pix", None, "site"),
        P("pix", "site"),
        P("site"),
        P(),
        P("site"),
        P("pix"),
        P("site"),
        P("pix"),
        P("pix"),
    )
    return jax.shard_map(
        local,
        mesh=mesh,
        in_specs=placed,
        out_specs=(P("site"), P("pix"), P("pix")),
        check_vma=False,
    )
```

profile of v0, /device:TPU:32, one launch (start us, length us, event | category | flops | bytes accessed | tf_op | source)
XLA Modules:
  0.0 284.1 jit_solution(2345974059912617424)
XLA Ops:
  0.6 0.0 copy-start
  0.6 0.7 convert_reduce_fusion.1
  1.3 0.7 convert_element_type.63
  2.1 7.3 %all-to-all-start = ((bf16[32,2,1]{1,2,0:T(2,128)(2,1)}), bf16[32,2,1]{1,2,0:T(2,128)(2,1)S(1)}, u32[]{:S(2)}, u32[]{:S(2)}) async-start(bf16[32,2,1]{1,2,0:T(2,128)(2,1)} %convert_element_type.63), calls=%async_computation | async-start | bytes 32768 | tf_op jit(solution)/shard_map/all_to_all | solution.py:41
  9.4 0.7 compare_bitcast_fusion
  10.1 0.0 copy-done
  10.1 0.9 convolution_bitcast_fusion
  11.0 0.1 copy.15
  11.1 6.3 %select_convert_fusion = bf16[64,256,128]{2,1,0:T(8,128)(2,1)} fusion(s32[64,256,128]{2,1,0:T(8,128)} %param.9, f32[256,128]{1,0:T(8,128)S(1)} %copy.15, pred[64]{0:T(512)(128)(4,1)S(1)} %compare_bitcast_fusion), kind=kLoop, calls=%fused_computation | loop fusion | flops 16777216 | bytes 12714048 | tf_op jit(solution)/shard_map/convert_element_type | solution.py:20
  17.3 0.0 copy-start.1
  17.3 0.0 all-to-all-done
  17.3 7.6 %all-to-all-start.1 = ((bf16[64,256,128]{2,1,0:T(8,128)(2,1)}), bf16[64,256,128]{2,1,0:T(8,128)(2,1)}, u32[]{:S(2)}, u32[]{:S(2)}) async-start(bf16[64,256,128]{2,1,0:T(8,128)(2,1)} %select_convert_fusion), calls=%async_computation.1 | async-start | bytes 8388608 | tf_op jit(solution)/shard_map/all_to_all | solution.py:40
  25.0 0.0 copy-done.1
  25.0 0.1 convert_reduce_fusion
  25.1 0.1 reshape.74
  25.2 0.2 fusion
  25.4 0.0 copy-start.4
  25.4 0.0 copy-start.6
  25.4 53.5 %all-to-all-done.1 = bf16[64,256,128]{2,1,0:T(8,128)(2,1)} async-done(((bf16[64,256,128]{2,1,0:T(8,128)(2,1)}), bf16[64,256,128]{2,1,0:T(8,128)(2,1)}, u32[]{:S(2)}, u32[]{:S(2)}) %all-to-all-start.1) | async-done | bytes 4194336 | tf_op jit(solution)/shard_map/all_to_all | solution.py:40
  78.9 2.8 convolution_bitcast_fusion.5
  81.8 2.9 %convolution_bitcast_fusion.6 = f32[1,128]{1,0:T(1,128)S(1)} fusion(bf16[64,256,128]{2,1,0:T(8,128)(2,1)} %all-to-all-done.1, bf16[64,256,1]{1,0,2:T(8,128)(2,1)S(1)} %fusion), kind=kOutput, calls=%fused_computation.11 | convolution fusion | flops 4194304 | bytes 4227584 | tf_op jit(solution)/shard_map/tkr,krj->tj/dot_general | solution.py:53
  84.7 63.2 %all-reduce = (f32[1,128]{1,0:T(1,128)S(1)}, f32[1,128]{1,0:T(1,128)S(1)}) all-reduce(f32[1,128]{1,0:T(1,128)S(1)} %convolution_bitcast_fusion.6, f32[1,128]{1,0:T(1,128)S(1)} %convolution_bitcast_fusion.5), channel_id=1, replica_groups=mesh['pix'=32,'site'=8] {'pix'}, use_global_device_ids=true, to_apply=%region_0.1 | all-reduce | flops 256 | bytes 2048 | tf_op jit(solution)/shard_map/psum | solution.py:56
  147.9 0.0 copy-done.4
  147.9 0.0 copy-done.6
  147.9 0.0 copy-start.2
  148.0 0.0 copy-start.3
  148.0 3.4 %fusion.21 = f32[1,64,256]{2,0,1:T(1,128)S(1)} fusion(bf16[64,256,128]{2,1,0:T(8,128)(2,1)} %all-to-all-done.1, f32[128]{0:T(128)S(1)} %copy-done.4, f32[128]{0:T(128)S(1)} %fusion.24), kind=kOutput, calls=%fused_computation.41 | convolution fusion | flops 4194688 | bytes 4260864 | tf_op jit(solution)/shard_map/krj,tj->tkr/dot_general | solution.py:59
  151.3 0.3 convolution_bitcast_fusion.3
  151.6 3.4 %fusion.31 = f32[1,64,256]{2,0,1:T(1,128)S(1)} fusion(bf16[64,256,128]{2,1,0:T(8,128)(2,1)} %all-to-all-done.1), kind=kOutput, calls=%fused_computation.53 | convolution fusion | flops 4194304 | bytes 4259840 | tf_op jit(solution)/shard_map/krj,tj->tkr/dot_general | solution.py:59
  155.0 0.3 convolution_bitcast_fusion.2
  155.3 29.4 %all-reduce.1 = (f32[16,1,256]{2,0,1:T(8,128)S(1)}, f32[4096]{0:T(1024)S(1)}) all-reduce(f32[16,1,256]{2,0,1:T(8,128)S(1)} %convolution_bitcast_fusion.2, f32[4096]{0:T(1024)S(1)} %bitcast.70), channel_id=1, replica_groups=mesh['pix'=32,'site'=8] {'site'}, use_global_device_ids=true, to_apply=%region_3.4 | all-reduce | flops 8192 | bytes 65536 | tf_op jit(solution)/shard_map/psum | solution.py:60
  184.7 0.0 copy-done.2
  184.7 0.0 copy-done.3
  184.8 0.2 fusion.1
  185.0 2.9 %convolution_bitcast_fusion.4 = f32[1,128]{1,0:T(1,128)S(1)} fusion(bf16[64,256,128]{2,1,0:T(8,128)(2,1)} %all-to-all-done.1, bf16[64,256,1]{1,0,2:T(8,128)(2,1)S(1)} %fusion.1), kind=kOutput, calls=%fused_computation.9 | convolution fusion | flops 4194304 | bytes 4227584 | tf_op jit(solution)/shard_map/tkr,krj->tj/dot_general | solution.py:53
  187.9 62.7 %psum.46 = f32[1,128]{1,0:T(1,128)S(1)} all-reduce(f32[1,128]{1,0:T(1,128)S(1)} %convolution_bitcast_fusion.4), channel_id=1, replica_groups=mesh['pix'=32,'site'=8] {'pix'}, use_global_device_ids=true, to_apply=%region_4.5 | all-reduce | flops 128 | bytes 1024 | tf_op jit(solution)/shard_map/psum | solution.py:56
  250.6 0.0 copy-start.5
  250.6 3.4 %fusion.17 = f32[1,64,256]{2,0,1:T(1,128)S(1)} fusion(bf16[64,256,128]{2,1,0:T(8,128)(2,1)} %all-to-all-done.1, f32[128]{0:T(128)S(1)} %fusion.24, f32[128]{0:T(128)S(1)} %fusion.20), kind=kOutput, calls=%fused_computation.36 | convolution fusion | flops 4194688 | bytes 4260864 | tf_op jit(solution)/shard_map/krj,tj->tkr/dot_general | solution.py:59
  254.0 0.3 convolution_bitcast_fusion.1
  254.3 29.2 %psum.47 = f32[4096]{0:T(1024)S(1)} all-reduce(f32[4096]{0:T(1024)S(1)} %bitcast.71), channel_id=1, replica_groups=mesh['pix'=32,'site'=8] {'site'}, use_global_device_ids=true, to_apply=%region_5.6 | all-reduce | flops 4096 | bytes 32768 | tf_op jit(solution)/shard_map/psum | solution.py:60
  283.4 0.6 add_maximum_fusion
  284.1 0.0 copy-done.5
  (10 shorter events, 0.1 us)
Async XLA Ops:
  0.6 9.4 %copy-start = (f32[16,256]{1,0:T(8,128)S(1)}, f32[16,256]{1,0:T(8,128)}, u32[]{:S(2)}) copy-start(f32[16,256]{1,0:T(8,128)} %param.12) | copy-start | bytes 49156
  2.1 15.3 %all-to-all-start = ((bf16[32,2,1]{1,2,0:T(2,128)(2,1)}), bf16[32,2,1]{1,2,0:T(2,128)(2,1)S(1)}, u32[]{:S(2)}, u32[]{:S(2)}) async-start(bf16[32,2,1]{1,2,0:T(2,128)(2,1)} %convert_element_type.63), calls=%async_computation | async-start | bytes 32768 | tf_op jit(solution)/shard_map/all_to_all | solution.py:41
  17.3 7.7 %copy-start.1 = (f32[4096]{0:T(1024)S(1)}, f32[4096]{0:T(1024)}, u32[]{:S(2)}) copy-start(f32[4096]{0:T(1024)} %param.17) | copy-start | bytes 49156
  17.3 61.6 %all-to-all-start.1 = ((bf16[64,256,128]{2,1,0:T(8,128)(2,1)}), bf16[64,256,128]{2,1,0:T(8,128)(2,1)}, u32[]{:S(2)}, u32[]{:S(2)}) async-start(bf16[64,256,128]{2,1,0:T(8,128)(2,1)} %select_convert_fusion), calls=%async_computation.1 | async-start | bytes 8388608 | tf_op jit(solution)/shard_map/all_to_all | solution.py:40
  25.4 122.6 %copy-start.4 = (f32[128]{0:T(128)S(1)}, f32[128]{0:T(128)}, u32[]{:S(2)}) copy-start(f32[128]{0:T(128)} %param.15) | copy-start | bytes 1540
  25.4 122.5 %copy-start.6 = (f32[128]{0:T(128)S(1)}, f32[128]{0:T(128)}, u32[]{:S(2)}) copy-start(f32[128]{0:T(128)} %param.13) | copy-start | bytes 1540
  147.9 36.8 %copy-start.2 = (f32[4096]{0:T(1024)S(1)}, f32[4096]{0:T(1024)}, u32[]{:S(2)}) copy-start(f32[4096]{0:T(1024)} %param.16) | copy-start | bytes 49156
  148.0 36.8 %copy-start.3 = (f32[4096]{0:T(1024)S(1)}, f32[4096]{0:T(1024)}, u32[]{:S(2)}) copy-start(f32[4096]{0:T(1024)} %param.14) | copy-start | bytes 49156
  250.6 33.5 %copy-start.5 = (f32[128]{0:T(128)}, f32[128]{0:T(128)S(1)}, u32[]{:S(2)}) copy-start(f32[128]{0:T(128)S(1)} %fusion.20) | copy-start | bytes 1540
where the time goes:
time: 285 us; the launch traced here: 284 us
  blocking collectives  184 us (65%)
  waiting for transfers between devices  53.5 us (19%)
  matrix products  20.9 us (7%)
  starting transfers between devices  15 us (5%)
  other arithmetic  8.33 us (3%)
    psum x2, blocking collectives, column_totals(): return lax.psum(partial_value, 'pix')  126 us
    psum x2, blocking collectives, row_totals(): return lax.psum(spread_rows(products), 'site')  58.6 us
    all_to_all x1, waiting for transfers between devices, local(): lax.all_to_all(coverage, 'pix', split_axis=0, concat_axis=0, tiled=True)  53.5 us
    dot_general x3, matrix products, row_totals(): jnp.einsum('krj,tj->tkr', tiles_here, values, preferred_element_type=jnp....  10.1 us
    dot_general x3, matrix products, column_totals(): jnp.einsum('tkr,krj->tj', selected, tiles_here, preferred_element_type=jn...  8.67 us
    all_to_all x1, starting transfers between devices, local(): lax.all_to_all(coverage, 'pix', split_axis=0, concat_axis=0, tiled=True)  7.64 us
    all_to_all x1, starting transfers between devices, local(): lax.all_to_all(position.astype(jnp.bfloat16), 'pix', split_axis=0, concat...  7.32 us
    convert_element_type x1, other arithmetic, build_tiles(): return jnp.where(filled[:, None, None], values, 0.0).astype(jnp.bfloat16)  6.26 us
  transfers between devices with their start and end apart: 2, of which 1 were waited for; matrix products, arithmetic and copies ran while one was open for 3% of the time, Pallas kernels for 0%

commit v1 on v0

--- a/solution.py
+++ b/solution.py
@@ -53,7 +53,7 @@
         partial_value = jnp.einsum(
             "tkr,krj->tj", selected, tiles_here, preferred_element_type=jnp.float32
         )
-        return lax.psum(partial_value, "pix")
+        return jnp.sum(lax.all_gather(partial_value, "pix"), axis=0)
 
     def row_totals(values):
         products = jnp.einsum("krj,tj->tkr", tiles_here, values, preferred_element_type=jnp.float32)

time: 285 us -> 219 us (0.77)
  blocking collectives: 184 us -> 117 us
    psum x2 -> x0, blocking collectives: 126 us -> none  [column_totals(): return lax.psum(partial_value, 'pix')]
    all_gather x0 -> x3, blocking collectives: none -> 58.7 us  [column_totals(): return jnp.sum(lax.all_gather(partial_value, 'pix'), axis=0)]
  transfers between devices with their start and end apart: 2 -> 2, of which waited for: 1 -> 1; matrix products, arithmetic and copies ran while one was open for 3% -> 4% of each run, Pallas kernels for 0% -> 0%
where the time goes in v1:
time: 219 us; the launch traced here: 217 us
  blocking collectives  117 us (53%)
  waiting for transfers between devices  53.5 us (24%)
  matrix products  20.9 us (10%)
  starting transfers between devices  15 us (7%)
  other arithmetic  8.48 us (4%)
    all_gather x3, blocking collectives, column_totals(): return jnp.sum(lax.all_gather(partial_value, 'pix'), axis=0)  58.7 us
    psum x2, blocking collectives, row_totals(): return lax.psum(spread_rows(products), 'site')  58.6 us
    all_to_all x1, waiting for transfers between devices, local(): lax.all_to_all(coverage, 'pix', split_axis=0, concat_axis=0, tiled=True)  53.5 us
    dot_general x3, matrix products, row_totals(): jnp.einsum('krj,tj->tkr', tiles_here, values, preferred_element_type=jnp....  10.1 us
    dot_general x3, matrix products, column_totals(): jnp.einsum('tkr,krj->tj', selected, tiles_here, preferred_element_type=jn...  8.65 us
    all_to_all x1, starting transfers between devices, local(): lax.all_to_all(coverage, 'pix', split_axis=0, concat_axis=0, tiled=True)  7.64 us
    all_to_all x1, starting transfers between devices, local(): lax.all_to_all(position.astype(jnp.bfloat16), 'pix', split_axis=0, concat...  7.32 us
    convert_element_type x1, other arithmetic, build_tiles(): return jnp.where(filled[:, None, None], values, 0.0).astype(jnp.bfloat16)  6.26 us
  transfers between devices with their start and end apart: 2, of which 1 were waited for; matrix products, arithmetic and copies ran while one was open for 4% of the time, Pallas kernels for 0%

profile of v1, /device:TPU:32, one launch (start us, length us, event | category | flops | bytes accessed | tf_op | source)
XLA Modules:
  0.0 217.0 jit_solution(5076095888013119459)
XLA Ops:
  0.6 0.0 copy-start
  0.6 0.7 convert_reduce_fusion.1
  1.3 0.7 convert_element_type.63
  2.1 7.3 %all-to-all-start = ((bf16[32,2,1]{1,2,0:T(2,128)(2,1)}), bf16[32,2,1]{1,2,0:T(2,128)(2,1)S(1)}, u32[]{:S(2)}, u32[]{:S(2)}) async-start(bf16[32,2,1]{1,2,0:T(2,128)(2,1)} %convert_element_type.63), calls=%async_computation | async-start | bytes 32768 | tf_op jit(solution)/shard_map/all_to_all | solution.py:41
  9.4 0.7 compare_bitcast_fusion
  10.1 0.0 copy-done
  10.1 0.9 convolution_bitcast_fusion
  11.0 0.1 copy.15
  11.1 6.3 %select_convert_fusion = bf16[64,256,128]{2,1,0:T(8,128)(2,1)} fusion(s32[64,256,128]{2,1,0:T(8,128)} %param.9, f32[256,128]{1,0:T(8,128)S(1)} %copy.15, pred[64]{0:T(512)(128)(4,1)S(1)} %compare_bitcast_fusion), kind=kLoop, calls=%fused_computation | loop fusion | flops 16777216 | bytes 12714048 | tf_op jit(solution)/shard_map/convert_element_type | solution.py:20
  17.3 0.0 copy-start.1
  17.3 0.0 all-to-all-done
  17.3 7.6 %all-to-all-start.1 = ((bf16[64,256,128]{2,1,0:T(8,128)(2,1)}), bf16[64,256,128]{2,1,0:T(8,128)(2,1)}, u32[]{:S(2)}, u32[]{:S(2)}) async-start(bf16[64,256,128]{2,1,0:T(8,128)(2,1)} %select_convert_fusion), calls=%async_computation.1 | async-start | bytes 8388608 | tf_op jit(solution)/shard_map/all_to_all | solution.py:40
  25.0 0.0 copy-done.1
  25.0 0.1 convert_reduce_fusion
  25.1 0.1 reshape.81
  25.2 0.2 fusion
  25.4 0.0 copy-start.4
  25.4 0.0 copy-start.6
  25.4 53.5 %all-to-all-done.1 = bf16[64,256,128]{2,1,0:T(8,128)(2,1)} async-done(((bf16[64,256,128]{2,1,0:T(8,128)(2,1)}), bf16[64,256,128]{2,1,0:T(8,128)(2,1)}, u32[]{:S(2)}, u32[]{:S(2)}) %all-to-all-start.1) | async-done | bytes 4194336 | tf_op jit(solution)/shard_map/all_to_all | solution.py:40
  78.9 2.9 %convolution_bitcast_fusion.6 = f32[1,1,128]{2,1,0:T(1,128)S(1)} fusion(bf16[64,256,128]{2,1,0:T(8,128)(2,1)} %all-to-all-done.1, bf16[64,256,1]{1,0,2:T(8,128)(2,1)S(1)} %fusion), kind=kOutput, calls=%fused_computation.11 | convolution fusion | flops 4194304 | bytes 4227584 | tf_op jit(solution)/shard_map/tkr,krj->tj/dot_general | solution.py:53
  81.9 18.3 %all-gather.3 = f32[32,1,128]{2,1,0:T(1,128)S(1)} all-gather(f32[1,1,128]{2,1,0:T(1,128)S(1)} %convolution_bitcast_fusion.6), channel_id=2, replica_groups=mesh['pix'=32,'site'=8] {'pix'}, dimensions={0}, use_global_device_ids=true | all-gather | bytes 16896 | tf_op jit(solution)/shard_map/all_gather | solution.py:56
  100.1 2.8 %convolution_bitcast_fusion.5 = f32[1,1,128]{2,1,0:T(1,128)S(1)} fusion(bf16[64,256,128]{2,1,0:T(8,128)(2,1)} %all-to-all-done.1), kind=kOutput, calls=%fused_computation.10 | convolution fusion | flops 4194304 | bytes 4194816 | tf_op jit(solution)/shard_map/tkr,krj->tj/dot_general | solution.py:53
  102.9 21.0 %all-gather.4 = f32[32,1,128]{2,1,0:T(1,128)S(1)} all-gather(f32[1,1,128]{2,1,0:T(1,128)S(1)} %convolution_bitcast_fusion.5), channel_id=3, replica_groups=mesh['pix'=32,'site'=8] {'pix'}, dimensions={0}, use_global_device_ids=true | all-gather | bytes 16896 | tf_op jit(solution)/shard_map/all_gather | solution.py:56
  124.0 0.1 reduce.3
  124.0 0.1 reduce.4
  124.1 0.0 copy-done.4
  124.1 0.0 copy-done.6
  124.1 0.0 copy-start.2
  124.1 0.0 copy-start.3
  124.1 3.4 %fusion.19 = f32[1,64,256]{2,0,1:T(1,128)S(1)} fusion(bf16[64,256,128]{2,1,0:T(8,128)(2,1)} %all-to-all-done.1, f32[128]{0:T(128)S(1)} %copy-done.4, f32[128]{0:T(128)S(1)} %subtract_clamp_fusion.3), kind=kOutput, calls=%fused_computation.38 | convolution fusion | flops 4194688 | bytes 4260864 | tf_op jit(solution)/shard_map/krj,tj->tkr/dot_general | solution.py:59
  127.5 0.3 convolution_bitcast_fusion.3
  127.8 3.4 %fusion.27 = f32[1,64,256]{2,0,1:T(1,128)S(1)} fusion(bf16[64,256,128]{2,1,0:T(8,128)(2,1)} %all-to-all-done.1), kind=kOutput, calls=%fused_computation.49 | convolution fusion | flops 4194304 | bytes 4259840 | tf_op jit(solution)/shard_map/krj,tj->tkr/dot_general | solution.py:59
  131.2 0.3 convolution_bitcast_fusion.2
  131.4 29.4 %all-reduce = (f32[16,1,256]{2,0,1:T(8,128)S(1)}, f32[4096]{0:T(1024)S(1)}) all-reduce(f32[16,1,256]{2,0,1:T(8,128)S(1)} %convolution_bitcast_fusion.2, f32[4096]{0:T(1024)S(1)} %bitcast.58), channel_id=1, replica_groups=mesh['pix'=32,'site'=8] {'site'}, use_global_device_ids=true, to_apply=%region_3.4 | all-reduce | flops 8192 | bytes 65536 | tf_op jit(solution)/shard_map/psum | solution.py:60
  160.9 0.0 copy-done.2
  160.9 0.0 copy-done.3
  160.9 0.2 fusion.1
  161.1 2.9 %convolution_bitcast_fusion.4 = f32[1,1,128]{2,1,0:T(1,128)S(1)} fusion(bf16[64,256,128]{2,1,0:T(8,128)(2,1)} %all-to-all-done.1, bf16[64,256,1]{1,0,2:T(8,128)(2,1)S(1)} %fusion.1), kind=kOutput, calls=%fused_computation.9 | convolution fusion | flops 4194304 | bytes 4227584 | tf_op jit(solution)/shard_map/tkr,krj->tj/dot_general | solution.py:53
  164.0 19.4 %all-gather.5 = f32[32,1,128]{2,1,0:T(1,128)S(1)} all-gather(f32[1,1,128]{2,1,0:T(1,128)S(1)} %convolution_bitcast_fusion.4), channel_id=4, replica_groups=mesh['pix'=32,'site'=8] {'pix'}, dimensions={0}, use_global_device_ids=true | all-gather | bytes 16896 | tf_op jit(solution)/shard_map/all_gather | solution.py:56
  183.5 0.1 reduce.5
  183.5 0.0 copy-start.5
  183.6 3.4 %fusion.17 = f32[1,64,256]{2,0,1:T(1,128)S(1)} fusion(bf16[64,256,128]{2,1,0:T(8,128)(2,1)} %all-to-all-done.1, f32[128]{0:T(128)S(1)} %subtract_clamp_fusion.3, f32[128]{0:T(128)S(1)} %subtract_clamp_fusion.2), kind=kOutput, calls=%fused_computation.36 | convolution fusion | flops 4194688 | bytes 4260864 | tf_op jit(solution)/shard_map/krj,tj->tkr/dot_general | solution.py:59
  186.9 0.3 convolution_bitcast_fusion.1
  187.2 29.1 %psum.23 = f32[4096]{0:T(1024)S(1)} all-reduce(f32[4096]{0:T(1024)S(1)} %bitcast.59), channel_id=1, replica_groups=mesh['pix'=32,'site'=8] {'site'}, use_global_device_ids=true, to_apply=%region_5.6 | all-reduce | flops 4096 | bytes 32768 | tf_op jit(solution)/shard_map/psum | solution.py:60
  216.4 0.6 add_maximum_fusion
  217.0 0.0 copy-done.5
  (10 shorter events, 0.1 us)
Async XLA Ops:
  0.6 9.4 %copy-start = (f32[16,256]{1,0:T(8,128)S(1)}, f32[16,256]{1,0:T(8,128)}, u32[]{:S(2)}) copy-start(f32[16,256]{1,0:T(8,128)} %param.12) | copy-start | bytes 49156
  2.1 15.3 %all-to-all-start = ((bf16[32,2,1]{1,2,0:T(2,128)(2,1)}), bf16[32,2,1]{1,2,0:T(2,128)(2,1)S(1)}, u32[]{:S(2)}, u32[]{:S(2)}) async-start(bf16[32,2,1]{1,2,0:T(2,128)(2,1)} %convert_element_type.63), calls=%async_computation | async-start | bytes 32768 | tf_op jit(solution)/shard_map/all_to_all | solution.py:41
  17.3 7.7 %copy-start.1 = (f32[4096]{0:T(1024)S(1)}, f32[4096]{0:T(1024)}, u32[]{:S(2)}) copy-start(f32[4096]{0:T(1024)} %param.17) | copy-start | bytes 49156
  17.3 61.6 %all-to-all-start.1 = ((bf16[64,256,128]{2,1,0:T(8,128)(2,1)}), bf16[64,256,128]{2,1,0:T(8,128)(2,1)}, u32[]{:S(2)}, u32[]{:S(2)}) async-start(bf16[64,256,128]{2,1,0:T(8,128)(2,1)} %select_convert_fusion), calls=%async_computation.1 | async-start | bytes 8388608 | tf_op jit(solution)/shard_map/all_to_all | solution.py:40
  25.4 98.7 %copy-start.4 = (f32[128]{0:T(128)S(1)}, f32[128]{0:T(128)}, u32[]{:S(2)}) copy-start(f32[128]{0:T(128)} %param.15) | copy-start | bytes 1540
  25.4 98.7 %copy-start.6 = (f32[128]{0:T(128)S(1)}, f32[128]{0:T(128)}, u32[]{:S(2)}) copy-start(f32[128]{0:T(128)} %param.13) | copy-start | bytes 1540
  124.1 36.8 %copy-start.2 = (f32[4096]{0:T(1024)S(1)}, f32[4096]{0:T(1024)}, u32[]{:S(2)}) copy-start(f32[4096]{0:T(1024)} %param.16) | copy-start | bytes 49156
  124.1 36.8 %copy-start.3 = (f32[4096]{0:T(1024)S(1)}, f32[4096]{0:T(1024)}, u32[]{:S(2)}) copy-start(f32[4096]{0:T(1024)} %param.14) | copy-start | bytes 49156
  183.5 33.4 %copy-start.5 = (f32[128]{0:T(128)}, f32[128]{0:T(128)S(1)}, u32[]{:S(2)}) copy-start(f32[128]{0:T(128)S(1)} %subtract_clamp_fusion.2) | copy-start | bytes 1540
